TPU v7x, 256 devices: a whole 4x4x8 slice. The times are simulated.
256 devices in a mesh: modes: 4 (over y_hi, core), space: 64 (over x, y_lo, z).
Axes of the slice: x: 4, y: 4 (y_hi: 2, y_lo: 2; y = y_hi * 2 + y_lo), z: 8, core: 2. Of those that a mesh axis runs over, the one named last changes fastest.
Arguments:
- thermal_deviation_iterate: float32 [4, 256, 256], P(None, 'space'), may hold values from -6 to 6
- volumetric_source_term: float32 [4, 256, 256], P(None, 'space'), may hold values from -6 to 6
- node_substance_label: int32 [4, 256, 256], P(None, 'space'), may hold values from 0 to 2
- spectral_table_lookup: int32 [40], P('modes'), may hold values from 0 to 63
- propagation_velocity_table: float32 [64], replicated, may hold values from 0.7 to 1
- specific_heat_table: float32 [64], replicated, may hold values from 0.5 to 2
- collision_frequency_table: float32 [64, 3], replicated, may hold values from 0.08 to 0.4
- ordinate_inclination: float32 [30], replicated, may hold values from 0.05 to 1.52
- ordinate_longitude: float32 [30], replicated, may hold values from -3.140625 to 3.140625
Outputs:
- new_temperature: float32 [4, 256, 256], P(None, 'space', 'modes')
- heat_flux: float32 [3, 4, 256, 256], P(None, None, 'space', 'modes')
All inputs are finite; a program needn't handle non-finite values.
Results may differ from a plain program's by a relative error of at most 0.000078.
Values sent between devices are 32-bit elements; how exact they have to be, the bound alone decides.
A program may use at most 64 MiB of HBM per device.

v0:
```python
import jax
import jax.numpy as jnp
from jax import lax
from jax.sharding import PartitionSpec as P

SPECTRAL_BINS = 40
SWEEPS = 3
CHEB = 16


def extended(block, sides, width):
    for axis, dim in sides:
        count = lax.axis_size(axis)
        forward = [(i, i + 1) for i in range(count - 1)]
        backward = [(target, source) for source, target in forward]
        low = lax.ppermute(
            lax.slice_in_dim(block, block.shape[dim] - width, None, axis=dim), axis, forward
        )
        high = lax.ppermute(lax.slice_in_dim(block, 0, width, axis=dim), axis, backward)
        block = jnp.concatenate([low, block, high], axis=dim)
    return block


def directions(ordinate_inclination, ordinate_longitude):
    along_x = jnp.cos(ordinate_inclination)
    along_y = jnp.sin(ordinate_inclination) * jnp.cos(ordinate_longitude)
    along_z = jnp.sin(ordinate_inclination) * jnp.sin(ordinate_longitude)
    return (
        jnp.concatenate([along_x, -along_x]),
        jnp.concatenate([along_y, -along_y]),
        jnp.concatenate([along_z, -along_z]),
    )


def diffuse_apply(padded_values, padded_kappa):
    center = padded_values[1:-1, 1:-1, 1:-1]
    kappa_here = padded_kappa[1:-1, 1:-1, 1:-1]
    slices = [
        (slice(1, -1), slice(None, -2), slice(1, -1)),
        (slice(1, -1), slice(2, None), slice(1, -1)),
        (slice(1, -1), slice(1, -1), slice(None, -2)),
        (slice(1, -1), slice(1, -1), slice(2, None)),
        (slice(None, -2), slice(1, -1), slice(1, -1)),
        (slice(2, None), slice(1, -1), slice(1, -1)),
    ]
    total = jnp.zeros_like(center)
    for where in slices:
        total = total + 0.5 * (kappa_here + padded_kappa[where]) * (center - padded_values[where])
    return center + total


def chebyshev(forcing_vector, operator, top):
    theta = (top + 1.0) / 2.0
    delta = (top - 1.0) / 2.0
    sigma = theta / delta

    def advance(index, carry):
        correction, equation_mismatch, direction, rho = carry
        correction = correction + direction
        equation_mismatch = equation_mismatch - operator(direction)
        rho_new = 1.0 / (2.0 * sigma - rho)
        direction = rho_new * rho * direction + 2.0 * rho_new / delta * equation_mismatch
        return (correction, equation_mismatch, direction, rho_new)

    start = (jnp.zeros_like(forcing_vector), forcing_vector, forcing_vector / theta, 1.0 / sigma)
    return lax.fori_loop(0, CHEB, advance, start)[0]


def cell_rates(rates, type_masks):
    return (
        rates[:, 0, None, None, None] * type_masks[0]
        + rates[:, 1, None, None, None] * type_masks[1]
        + rates[:, 2, None, None, None] * type_masks[2]
    )[:, None]


def on_device(
    thermal_deviation_iterate,
    volumetric_source_term,
    node_substance_label,
    spectral_table_lookup,
    propagation_velocity_table,
    specific_heat_table,
    collision_frequency_table,
    ordinate_inclination,
    ordinate_longitude,
):
    pointwise_spectral_value = spectral_table_lookup.shape[0]
    tiled_extent = thermal_deviation_iterate.shape[2] // lax.axis_size("modes")
    table_rows = propagation_velocity_table.shape[0]
    onehot = (
        spectral_table_lookup[:, None] == jnp.arange(table_rows, dtype=jnp.int32)[None, :]
    ).astype(jnp.float32)
    highest = lax.Precision.HIGHEST
    velocity = jnp.dot(onehot, propagation_velocity_table, precision=highest)
    first_freq = lax.axis_index("modes") * pointwise_spectral_value
    spectral = (
        (first_freq + jnp.arange(pointwise_spectral_value, dtype=jnp.int32)).astype(jnp.float32)
        + 1.0
    ) / SPECTRAL_BINS
    specific_thermal_storage = jnp.dot(onehot, specific_heat_table, precision=highest) * spectral
    rates = jnp.dot(onehot, collision_frequency_table, precision=highest)
    part_rate = jnp.sum(specific_thermal_storage[:, None] * rates, axis=0)
    part_cond = jnp.sum(
        (specific_thermal_storage * velocity * velocity)[:, None] / (3.0 * rates), axis=0
    )
    rate_total, cond_total = lax.psum((part_rate, part_cond), "modes")
    along_x, along_y, along_z = directions(ordinate_inclination, ordinate_longitude)
    half_dir = ordinate_inclination.shape[0]
    masks = [(node_substance_label == kind).astype(jnp.float32) for kind in range(3)]
    node_collision_frequency = cell_rates(rates, masks)
    speed_x = velocity[:, None] * along_x[None, :]
    speed_y = velocity[:, None] * along_y[None, :]
    speed_z = velocity[:, None] * along_z[None, :]

    def expand(coef):
        return coef[:, :, None, None, None]

    abs_sum = jnp.abs(along_x) + jnp.abs(along_y) + jnp.abs(along_z)
    ordinate_weighted_sum = 2 * half_dir
    denom = expand(velocity[:, None] * abs_sum[None, :]) + node_collision_frequency
    equilibrium_emission = specific_thermal_storage[:, None, None, None, None] * (
        node_collision_frequency * thermal_deviation_iterate + volumetric_source_term
    )
    iteration_bundle = jnp.broadcast_to(
        specific_thermal_storage[:, None, None, None, None] * thermal_deviation_iterate,
        (pointwise_spectral_value, ordinate_weighted_sum) + thermal_deviation_iterate.shape,
    )
    forward_x = expand(jnp.maximum(speed_x, 0.0))
    backward_x = expand(jnp.maximum(-speed_x, 0.0))
    forward_y = expand(jnp.maximum(speed_y, 0.0))
    backward_y = expand(jnp.maximum(-speed_y, 0.0))
    forward_z = expand(jnp.maximum(speed_z, 0.0))
    backward_z = expand(jnp.maximum(-speed_z, 0.0))
    for sweep_index in range(SWEEPS):
        xpad = extended(iteration_bundle, (("space", 3),), 1)
        xterm = forward_x * xpad[:, :, :, :-2] + backward_x * xpad[:, :, :, 2:]
        ypad = jnp.pad(iteration_bundle, ((0, 0), (0, 0), (0, 0), (0, 0), (1, 1)))
        zpad = jnp.pad(iteration_bundle, ((0, 0), (0, 0), (1, 1), (0, 0), (0, 0)))
        yterm = forward_y * ypad[..., :-2] + backward_y * ypad[..., 2:]
        zterm = forward_z * zpad[:, :, :-2] + backward_z * zpad[:, :, 2:]
        iteration_bundle = (xterm + yterm + zterm + equilibrium_emission) / denom
    summed = jnp.sum(iteration_bundle, axis=1)
    numer = jnp.sum(node_collision_frequency[:, 0] * summed, axis=0) / ordinate_weighted_sum
    fluxes = [
        jnp.einsum("fd,fdpxy->pxy", coef, iteration_bundle, precision=highest)
        / ordinate_weighted_sum
        for coef in (speed_x, speed_y, speed_z)
    ]
    moments = jnp.stack([numer] + fluxes)
    leading_entry_index = lax.axis_index("modes") * tiled_extent
    whole_moments = lax.psum(moments, "modes")
    tile_moments = lax.dynamic_slice_in_dim(whole_moments, leading_entry_index, tiled_extent, 3)
    tile_types = lax.dynamic_slice_in_dim(
        node_substance_label, leading_entry_index, tiled_extent, 2
    )
    tiled_thermal_deviation = lax.dynamic_slice_in_dim(
        thermal_deviation_iterate, leading_entry_index, tiled_extent, 2
    )
    tile_masks = [(tile_types == kind).astype(jnp.float32) for kind in range(3)]
    conduct = cond_total / rate_total
    tile_kappa = (
        conduct[0] * tile_masks[0] + conduct[1] * tile_masks[1] + conduct[2] * tile_masks[2]
    )
    cell_total = (
        rate_total[0] * tile_masks[0]
        + rate_total[1] * tile_masks[1]
        + rate_total[2] * tile_masks[2]
    )
    hemisphere_ordinates = tile_moments[0] / cell_total
    top = 1.0 + 12.0 * jnp.max(conduct)
    forcing_vector = hemisphere_ordinates - tiled_thermal_deviation
    kappa_edges = extended(tile_kappa, (("modes", 2), ("space", 1)), 1)
    padded_kappa = jnp.pad(kappa_edges, ((1, 1), (0, 0), (0, 0)))

    def apply_tile(direction):
        edges = extended(direction, (("modes", 2), ("space", 1)), 1)
        return diffuse_apply(jnp.pad(edges, ((1, 1), (0, 0), (0, 0))), padded_kappa)

    correction = chebyshev(forcing_vector, apply_tile, top)
    return (hemisphere_ordinates + correction, tile_moments[1:4])


def solution(mesh):
    placed = (
        P(None, "space", None),
        P(None, "space", None),
        P(None, "space", None),
        P("modes"),
        P(),
        P(),
        P(),
        P(),
        P(),
    )
    return jax.shard_map(
        on_device,
        mesh=mesh,
        in_specs=placed,
        out_specs=(P(None, "space", "modes"), P(None, None, "space", "modes")),
        check_vma=False,
    )
```

profile of v0, /device:TPU:22, one launch (start us, length us, event | category | flops | bytes accessed | tf_op | source)
XLA Modules:
  0.0 737.0 jit_solution(17118505579713076804)
XLA Ops:
  16.3 6.8 collective-permute-start.5
  24.9 49.3 %collective-permute-done.4 = f32[10,60,4,1,256]{4,2,3,1,0:T(4,128)S(1)} collective-permute-done((f32[10,60,4,1,256]{4,2,3,1,0:T(4,128)S(1)}, f32[10,60,4,1,256]{4,2,3,1,0:T(4,128)S(1)}, u32[]{:S(2)}, u32[]{:S(2)}) %collective-permute-start.4) | collective-permute-done | bytes 2457632 | tf_op jit(solution)/shard_map/ppermute | solution.py:16
  77.2 6.3 broadcast_in_dim.7
  83.5 31.0 %add_divide_fusion.2 = f32[10,60,4,4,256]{4,2,3,1,0:T(4,128)} fusion(f32[10,60,4,4,256]{4,2,3,1,0:T(4,128)} %broadcast_in_dim.7, f32[10,60,4,1,256]{4,2,3,1,0:T(4,128)} %copy-done.3, f32[10,60,4,1,256]{4,2,3,1,0:T(4,128)S(1)} %collective-permute-done.4, f32[10,4,4,256]{3,1,2,0:T(4,128)S(1)} %copy.13, f32[10,60]{1,0:T(8,128)S(1)} %get-tuple-element.267, ...), kind=kLoop, calls=%fused_computation.49 | loop fusion | flops 39321600 | bytes 24920480 | tf_op jit(solution)/shard_map/div | solution.py:142
  119.7 7.4 %collective-permute-start.7 = (f32[10,60,4,1,256]{4,2,3,1,0:T(4,128)S(1)}, f32[10,60,4,1,256]{4,2,3,1,0:T(4,128)}, u32[]{:S(2)}, u32[]{:S(2)}) collective-permute-start(f32[10,60,4,1,256]{4,2,3,1,0:T(4,128)S(1)} %get-tuple-element.232), channel_id=1, source_target_pairs={{1,0},{2,1},{3,2},{4,3},{5,4},{6,5},{7,6},{8,7},{9,8},{10,9},{11,1... | collective-permute-start | bytes 7372808 | tf_op jit(solution)/shard_map/ppermute | solution.py:19
  127.1 50.6 %collective-permute-done.6 = f32[10,60,4,1,256]{4,2,3,1,0:T(4,128)S(1)} collective-permute-done((f32[10,60,4,1,256]{4,2,3,1,0:T(4,128)S(1)}, f32[10,60,4,1,256]{4,2,3,1,0:T(4,128)S(1)}, u32[]{:S(2)}, u32[]{:S(2)}) %collective-permute-start.6) | collective-permute-done | bytes 2457632 | tf_op jit(solution)/shard_map/ppermute | solution.py:16
  178.8 31.0 %add_divide_fusion.1 = f32[10,60,4,4,256]{4,2,3,1,0:T(4,128)} fusion(f32[10,60,4,4,256]{4,2,3,1,0:T(4,128)} %add_divide_fusion.2, f32[10,60,4,1,256]{4,2,3,1,0:T(4,128)} %collective-permute-done.7, f32[10,60,4,1,256]{4,2,3,1,0:T(4,128)S(1)} %collective-permute-done.6, f32[10,4,4,256]{3,1,2,0:T(4,128)S(1)} %copy.13, f32[10,60]{1,0:T(8,128)S(1)} %get-tuple-element.267, ...), kind=kLoop, calls=%fused_computation.48 | loop fusion | flops 39321600 | bytes 24920480 | tf_op jit(solution)/shard_map/div | solution.py:142
  209.8 5.6 fusion.91
  217.5 7.3 collective-permute-start.9
  224.8 47.1 %all-reduce.8 = (f32[3]{0:T(128)S(1)}, f32[3]{0:T(128)S(1)}) all-reduce(f32[3]{0:T(128)S(1)} %get-tuple-element.176, f32[3]{0:T(128)S(1)} %get-tuple-element.175), channel_id=1, replica_groups=mesh['modes'=4,'space'=64] {'modes'}, use_global_device_ids=true, to_apply=%region_4.5 | all-reduce | flops 6 | bytes 48 | tf_op jit(solution)/shard_map/psum | solution.py:107
  277.0 5.1 collective-permute-start.11
  285.5 8.7 %collective-permute-start.13 = (f32[4,1,66]{2,1,0:T(1,128)S(1)}, f32[4,1,66]{2,1,0:T(1,128)S(1)}, u32[]{:S(2)}, u32[]{:S(2)}) collective-permute-start(f32[4,1,66]{2,1,0:T(1,128)S(1)} %get-tuple-element.241), channel_id=1, source_target_pairs={{1,0},{2,1},{3,2},{4,3},{5,4},{6,5},{7,6},{8,7},{9,8},{10,9},{11,1... | collective-permute-start | bytes 3176 | tf_op jit(solution)/shard_map/ppermute | solution.py:19
  296.5 31.8 %fusion.87 = (f32[10,4,4,256]{3,1,2,0:T(4,128)S(1)}, f32[10,60,4,4,256]{4,2,3,1,0:T(4,128)}) fusion(f32[10,4,4,256]{3,1,2,0:T(4,128)S(1)} %copy.13, f32[10,60]{1,0:T(8,128)S(1)} %get-tuple-element.267, f32[10,4,4,256]{3,1,2,0:T(4,128)S(1)} %copy.12, f32[10,60]{1,0:T(8,128)S(1)} %get-tuple-element.269, f32[10,60,4,4,256]{4,2,3,1,0:T(4,128)} %add_divide_fusion.1, ...), kind=kLoop, calls=%fused_computation.194 | loop fusion | flops 41738240 | bytes 25084320 | tf_op jit(solution)/shard_map/reduce_sum | solution.py:143
  328.4 15.9 %fusion.22 = f32[1,4,4,256,1]{3,0,4,2,1:T(1,128)S(1)} fusion(f32[10,60,4,4,256]{4,2,3,1,0:T(4,128)} %get-tuple-element.216, f32[10,60,1,1,1]{1,0,2,3,4:T(8,128)S(1)} %get-tuple-element.256), kind=kOutput, calls=%fused_computation.58 | convolution fusion | flops 29491200 | bytes 9849184 | tf_op jit(solution)/shard_map/fd,fdpxy->pxy/dot_general | solution.py:146
  344.3 9.9 %fusion.20 = f32[1,4,4,256,1]{3,0,4,2,1:T(1,128)S(1)} fusion(f32[10,60,4,4,256]{4,2,3,1,0:T(4,128)S(1)} %copy-done.2, f32[10,60,1,1,1]{1,0,2,3,4:T(8,128)S(1)} %get-tuple-element.273), kind=kOutput, calls=%fused_computation.56 | convolution fusion | flops 29491200 | bytes 9849184 | tf_op jit(solution)/shard_map/fd,fdpxy->pxy/dot_general | solution.py:146
  354.2 9.7 %fusion.18 = f32[1,4,4,256,1]{3,0,4,2,1:T(1,128)S(1)} fusion(f32[10,60,4,4,256]{4,2,3,1,0:T(4,128)S(1)} %copy-done.2, f32[10,60,1,1,1]{1,0,2,3,4:T(8,128)S(1)} %get-tuple-element.270), kind=kOutput, calls=%fused_computation.54 | convolution fusion | flops 29491200 | bytes 9849184 | tf_op jit(solution)/shard_map/fd,fdpxy->pxy/dot_general | solution.py:146
  364.7 41.6 %all-reduce.11.cloned.1.call-done = f32[4,4,4,256]{3,2,1,0:T(4,128)} async-done(((f32[4,4,4,256]{3,2,1,0:T(4,128)}), f32[4,4,4,256]{3,2,1,0:T(4,128)}) %all-reduce.11.cloned.1.call-update) | async-done | bytes 65552 | tf_op jit(solution)/shard_map/psum | solution.py:152
  406.3 4.5 slice_add_fusion
  410.8 314.6 %while.19 = (s32[]{:T(128)}, f32[4,4,64]{2,1,0:T(4,128)S(1)}, f32[4,4,64]{2,1,0:T(4,128)S(1)}, f32[4,4,64]{2,1,0:T(4,128)S(1)}, f32[]{:T(128)}, /*index=5*/f32[4...) while((s32[]{:T(128)}, f32[4,4,64]{2,1,0:T(4,128)S(1)}, ...), condition=%wide.region_9.10_spmd.clone, body=%wide.region_8.9_spmd.clone.sunk | while | flops 68488 | bytes 103667 | solution.py:66
  410.9 4.9 collective-permute-start
  417.8 4.5 collective-permute-done.1
  422.4 6.1 collective-permute-start.2
  430.6 6.4 collective-permute-done.3
  441.7 4.0 collective-permute-done.1
  451.8 4.4 collective-permute-done.3
  460.9 4.0 collective-permute-done.1
  471.0 4.4 collective-permute-done.3
  480.1 4.0 collective-permute-done.1
  490.2 4.4 collective-permute-done.3
  499.3 4.0 collective-permute-done.1
  509.4 4.4 collective-permute-done.3
  518.6 4.0 collective-permute-done.1
  528.7 4.4 collective-permute-done.3
  537.8 4.0 collective-permute-done.1
  547.9 4.4 collective-permute-done.3
  557.0 4.0 collective-permute-done.1
  567.1 4.4 collective-permute-done.3
  576.2 4.0 collective-permute-done.1
  586.3 4.4 collective-permute-done.3
  595.4 4.0 collective-permute-done.1
  605.5 4.4 collective-permute-done.3
  614.6 4.0 collective-permute-done.1
  624.7 4.4 collective-permute-done.3
  643.9 4.4 collective-permute-done.3
  663.1 4.4 collective-permute-done.3
  682.3 4.4 collective-permute-done.3
  701.6 4.4 collective-permute-done.3
  720.8 4.4 collective-permute-done.3
  (257 shorter events, 219.8 us)
Async XLA Ops:
  7.2 399.2 %all-reduce.11.cloned.1.call-start = ((), (), s32[]{:S(2)}) async-start(), calls=%async_computation | async-start | bytes 131072 | tf_op jit(solution)/shard_map/psum | solution.py:152
  12.1 62.1 %collective-permute-start.4 = (f32[10,60,4,1,256]{4,2,3,1,0:T(4,128)S(1)}, f32[10,60,4,1,256]{4,2,3,1,0:T(4,128)S(1)}, u32[]{:S(2)}, u32[]{:S(2)}) collective-permute-start(f32[10,60,4,1,256]{4,2,3,1,0:T(4,128)S(1)} %broadcast_in_dim.6), channel_id=1, source_target_pairs={{0,1},{1,2},{2,3},{3,4},{4,5},{5,6},{6,7},{7,8},{8,9},{9,10},{10,1... | collective-permute-start | bytes 7372808 | tf_op jit(solution)/shard_map/ppermute | solution.py:16
  16.3 59.4 %collective-permute-start.5 = (f32[10,60,4,1,256]{4,2,3,1,0:T(4,128)S(1)}, f32[10,60,4,1,256]{4,2,3,1,0:T(4,128)S(1)}, u32[]{:S(2)}, u32[]{:S(2)}) collective-permute-start(f32[10,60,4,1,256]{4,2,3,1,0:T(4,128)S(1)} %broadcast_in_dim.8), channel_id=1, source_target_pairs={{1,0},{2,1},{3,2},{4,3},{5,4},{6,5},{7,6},{8,7},{9,8},{10,9},{11,1... | collective-permute-start | bytes 7372808 | tf_op jit(solution)/shard_map/ppermute | solution.py:19
  117.8 59.9 %collective-permute-start.6 = (f32[10,60,4,1,256]{4,2,3,1,0:T(4,128)S(1)}, f32[10,60,4,1,256]{4,2,3,1,0:T(4,128)S(1)}, u32[]{:S(2)}, u32[]{:S(2)}) collective-permute-start(f32[10,60,4,1,256]{4,2,3,1,0:T(4,128)S(1)} %get-tuple-element.231), channel_id=1, source_target_pairs={{0,1},{1,2},{2,3},{3,4},{4,5},{5,6},{6,7},{7,8},{8,9},{9,10},{10,1... | collective-permute-start | bytes 7372808 | tf_op jit(solution)/shard_map/ppermute | solution.py:16
  119.7 59.1 %collective-permute-start.7 = (f32[10,60,4,1,256]{4,2,3,1,0:T(4,128)S(1)}, f32[10,60,4,1,256]{4,2,3,1,0:T(4,128)}, u32[]{:S(2)}, u32[]{:S(2)}) collective-permute-start(f32[10,60,4,1,256]{4,2,3,1,0:T(4,128)S(1)} %get-tuple-element.232), channel_id=1, source_target_pairs={{1,0},{2,1},{3,2},{4,3},{5,4},{6,5},{7,6},{8,7},{9,8},{10,9},{11,1... | collective-permute-start | bytes 7372808 | tf_op jit(solution)/shard_map/ppermute | solution.py:19
  215.4 81.1 %collective-permute-start.8 = (f32[10,60,4,1,256]{4,2,3,1,0:T(4,128)}, f32[10,60,4,1,256]{4,2,3,1,0:T(4,128)S(1)}, u32[]{:S(2)}, u32[]{:S(2)}) collective-permute-start(f32[10,60,4,1,256]{4,2,3,1,0:T(4,128)} %get-tuple-element.229), channel_id=1, source_target_pairs={{0,1},{1,2},{2,3},{3,4},{4,5},{5,6},{6,7},{7,8},{8,9},{9,10},{10,1... | collective-permute-start | bytes 7372808 | tf_op jit(solution)/shard_map/ppermute | solution.py:16
  217.5 79.0 %collective-permute-start.9 = (f32[10,60,4,1,256]{4,2,3,1,0:T(4,128)}, f32[10,60,4,1,256]{4,2,3,1,0:T(4,128)}, u32[]{:S(2)}, u32[]{:S(2)}) collective-permute-start(f32[10,60,4,1,256]{4,2,3,1,0:T(4,128)} %get-tuple-element.230), channel_id=1, source_target_pairs={{1,0},{2,1},{3,2},{4,3},{5,4},{6,5},{7,6},{8,7},{9,8},{10,9},{11,1... | collective-permute-start | bytes 7372808 | tf_op jit(solution)/shard_map/ppermute | solution.py:19
  275.1 7.1 collective-permute-start.10
  277.0 6.5 collective-permute-start.11
  283.6 12.7 %collective-permute-start.12 = (f32[4,1,66]{2,1,0:T(1,128)S(1)}, f32[4,1,66]{2,1,0:T(1,128)S(1)}, u32[]{:S(2)}, u32[]{:S(2)}) collective-permute-start(f32[4,1,66]{2,1,0:T(1,128)S(1)} %get-tuple-element.242), channel_id=1, source_target_pairs={{0,1},{1,2},{2,3},{3,4},{4,5},{5,6},{6,7},{7,8},{8,9},{9,10},{10,1... | collective-permute-start | bytes 3176 | tf_op jit(solution)/shard_map/ppermute | solution.py:16
  285.5 10.8 %collective-permute-start.13 = (f32[4,1,66]{2,1,0:T(1,128)S(1)}, f32[4,1,66]{2,1,0:T(1,128)S(1)}, u32[]{:S(2)}, u32[]{:S(2)}) collective-permute-start(f32[4,1,66]{2,1,0:T(1,128)S(1)} %get-tuple-element.241), channel_id=1, source_target_pairs={{1,0},{2,1},{3,2},{4,3},{5,4},{6,5},{7,6},{8,7},{9,8},{10,9},{11,1... | collective-permute-start | bytes 3176 | tf_op jit(solution)/shard_map/ppermute | solution.py:19
  410.9 6.8 collective-permute-start
  415.9 6.5 collective-permute-start.1
  422.4 8.2 %collective-permute-start.2 = (f32[4,1,66]{2,1,0:T(1,128)S(1)}, f32[4,1,66]{2,1,0:T(1,128)S(1)}, u32[]{:S(2)}, u32[]{:S(2)}) collective-permute-start(f32[4,1,66]{2,1,0:T(1,128)S(1)} %get-tuple-element.376), channel_id=1, source_target_pairs={{1,0},{2,1},{3,2},{4,3},{5,4},{6,5},{7,6},{8,7},{9,8},{10,9},{11,1... | collective-permute-start | bytes 3176 | tf_op jit(solution)/shard_map/while/body/eval_jaxpr/ppermute | solution.py:19
  428.6 8.5 %collective-permute-start.3 = (f32[4,1,66]{2,1,0:T(1,128)S(1)}, f32[4,1,66]{2,1,0:T(1,128)S(1)}, u32[]{:S(2)}, u32[]{:S(2)}) collective-permute-start(f32[4,1,66]{2,1,0:T(1,128)S(1)} %get-tuple-element.377), channel_id=1, source_target_pairs={{0,1},{1,2},{2,3},{3,4},{4,5},{5,6},{6,7},{7,8},{8,9},{9,10},{10,1... | collective-permute-start | bytes 3176 | tf_op jit(solution)/shard_map/while/body/eval_jaxpr/ppermute | solution.py:16
  439.3 6.5 collective-permute-start.1
  447.8 8.5 %collective-permute-start.3 = (f32[4,1,66]{2,1,0:T(1,128)S(1)}, f32[4,1,66]{2,1,0:T(1,128)S(1)}, u32[]{:S(2)}, u32[]{:S(2)}) collective-permute-start(f32[4,1,66]{2,1,0:T(1,128)S(1)} %get-tuple-element.377), channel_id=1, source_target_pairs={{0,1},{1,2},{2,3},{3,4},{4,5},{5,6},{6,7},{7,8},{8,9},{9,10},{10,1... | collective-permute-start | bytes 3176 | tf_op jit(solution)/shard_map/while/body/eval_jaxpr/ppermute | solution.py:16
  458.5 6.5 collective-permute-start.1
  465.1 6.0 collective-permute-start.2
  467.0 8.5 %collective-permute-start.3 = (f32[4,1,66]{2,1,0:T(1,128)S(1)}, f32[4,1,66]{2,1,0:T(1,128)S(1)}, u32[]{:S(2)}, u32[]{:S(2)}) collective-permute-start(f32[4,1,66]{2,1,0:T(1,128)S(1)} %get-tuple-element.377), channel_id=1, source_target_pairs={{0,1},{1,2},{2,3},{3,4},{4,5},{5,6},{6,7},{7,8},{8,9},{9,10},{10,1... | collective-permute-start | bytes 3176 | tf_op jit(solution)/shard_map/while/body/eval_jaxpr/ppermute | solution.py:16
  477.7 6.5 collective-permute-start.1
  486.2 8.5 %collective-permute-start.3 = (f32[4,1,66]{2,1,0:T(1,128)S(1)}, f32[4,1,66]{2,1,0:T(1,128)S(1)}, u32[]{:S(2)}, u32[]{:S(2)}) collective-permute-start(f32[4,1,66]{2,1,0:T(1,128)S(1)} %get-tuple-element.377), channel_id=1, source_target_pairs={{0,1},{1,2},{2,3},{3,4},{4,5},{5,6},{6,7},{7,8},{8,9},{9,10},{10,1... | collective-permute-start | bytes 3176 | tf_op jit(solution)/shard_map/while/body/eval_jaxpr/ppermute | solution.py:16
  496.9 6.5 collective-permute-start.1
  505.4 8.5 %collective-permute-start.3 = (f32[4,1,66]{2,1,0:T(1,128)S(1)}, f32[4,1,66]{2,1,0:T(1,128)S(1)}, u32[]{:S(2)}, u32[]{:S(2)}) collective-permute-start(f32[4,1,66]{2,1,0:T(1,128)S(1)} %get-tuple-element.377), channel_id=1, source_target_pairs={{0,1},{1,2},{2,3},{3,4},{4,5},{5,6},{6,7},{7,8},{8,9},{9,10},{10,1... | collective-permute-start | bytes 3176 | tf_op jit(solution)/shard_map/while/body/eval_jaxpr/ppermute | solution.py:16
  516.1 6.5 collective-permute-start.1
  522.7 6.0 collective-permute-start.2
  524.6 8.5 %collective-permute-start.3 = (f32[4,1,66]{2,1,0:T(1,128)S(1)}, f32[4,1,66]{2,1,0:T(1,128)S(1)}, u32[]{:S(2)}, u32[]{:S(2)}) collective-permute-start(f32[4,1,66]{2,1,0:T(1,128)S(1)} %get-tuple-element.377), channel_id=1, source_target_pairs={{0,1},{1,2},{2,3},{3,4},{4,5},{5,6},{6,7},{7,8},{8,9},{9,10},{10,1... | collective-permute-start | bytes 3176 | tf_op jit(solution)/shard_map/while/body/eval_jaxpr/ppermute | solution.py:16
  535.3 6.5 collective-permute-start.1
  543.8 8.5 %collective-permute-start.3 = (f32[4,1,66]{2,1,0:T(1,128)S(1)}, f32[4,1,66]{2,1,0:T(1,128)S(1)}, u32[]{:S(2)}, u32[]{:S(2)}) collective-permute-start(f32[4,1,66]{2,1,0:T(1,128)S(1)} %get-tuple-element.377), channel_id=1, source_target_pairs={{0,1},{1,2},{2,3},{3,4},{4,5},{5,6},{6,7},{7,8},{8,9},{9,10},{10,1... | collective-permute-start | bytes 3176 | tf_op jit(solution)/shard_map/while/body/eval_jaxpr/ppermute | solution.py:16
  554.5 6.5 collective-permute-start.1
  563.0 8.5 %collective-permute-start.3 = (f32[4,1,66]{2,1,0:T(1,128)S(1)}, f32[4,1,66]{2,1,0:T(1,128)S(1)}, u32[]{:S(2)}, u32[]{:S(2)}) collective-permute-start(f32[4,1,66]{2,1,0:T(1,128)S(1)} %get-tuple-element.377), channel_id=1, source_target_pairs={{0,1},{1,2},{2,3},{3,4},{4,5},{5,6},{6,7},{7,8},{8,9},{9,10},{10,1... | collective-permute-start | bytes 3176 | tf_op jit(solution)/shard_map/while/body/eval_jaxpr/ppermute | solution.py:16
  573.8 6.5 collective-permute-start.1
  580.3 6.0 collective-permute-start.2
  582.2 8.5 %collective-permute-start.3 = (f32[4,1,66]{2,1,0:T(1,128)S(1)}, f32[4,1,66]{2,1,0:T(1,128)S(1)}, u32[]{:S(2)}, u32[]{:S(2)}) collective-permute-start(f32[4,1,66]{2,1,0:T(1,128)S(1)} %get-tuple-element.377), channel_id=1, source_target_pairs={{0,1},{1,2},{2,3},{3,4},{4,5},{5,6},{6,7},{7,8},{8,9},{9,10},{10,1... | collective-permute-start | bytes 3176 | tf_op jit(solution)/shard_map/while/body/eval_jaxpr/ppermute | solution.py:16
  593.0 6.5 collective-permute-start.1
  601.5 8.5 %collective-permute-start.3 = (f32[4,1,66]{2,1,0:T(1,128)S(1)}, f32[4,1,66]{2,1,0:T(1,128)S(1)}, u32[]{:S(2)}, u32[]{:S(2)}) collective-permute-start(f32[4,1,66]{2,1,0:T(1,128)S(1)} %get-tuple-element.377), channel_id=1, source_target_pairs={{0,1},{1,2},{2,3},{3,4},{4,5},{5,6},{6,7},{7,8},{8,9},{9,10},{10,1... | collective-permute-start | bytes 3176 | tf_op jit(solution)/shard_map/while/body/eval_jaxpr/ppermute | solution.py:16
  612.2 6.5 collective-permute-start.1
  620.7 8.5 %collective-permute-start.3 = (f32[4,1,66]{2,1,0:T(1,128)S(1)}, f32[4,1,66]{2,1,0:T(1,128)S(1)}, u32[]{:S(2)}, u32[]{:S(2)}) collective-permute-start(f32[4,1,66]{2,1,0:T(1,128)S(1)} %get-tuple-element.377), channel_id=1, source_target_pairs={{0,1},{1,2},{2,3},{3,4},{4,5},{5,6},{6,7},{7,8},{8,9},{9,10},{10,1... | collective-permute-start | bytes 3176 | tf_op jit(solution)/shard_map/while/body/eval_jaxpr/ppermute | solution.py:16
  631.4 6.5 collective-permute-start.1
  639.9 8.5 %collective-permute-start.3 = (f32[4,1,66]{2,1,0:T(1,128)S(1)}, f32[4,1,66]{2,1,0:T(1,128)S(1)}, u32[]{:S(2)}, u32[]{:S(2)}) collective-permute-start(f32[4,1,66]{2,1,0:T(1,128)S(1)} %get-tuple-element.377), channel_id=1, source_target_pairs={{0,1},{1,2},{2,3},{3,4},{4,5},{5,6},{6,7},{7,8},{8,9},{9,10},{10,1... | collective-permute-start | bytes 3176 | tf_op jit(solution)/shard_map/while/body/eval_jaxpr/ppermute | solution.py:16
  650.6 6.5 collective-permute-start.1
  659.1 8.5 %collective-permute-start.3 = (f32[4,1,66]{2,1,0:T(1,128)S(1)}, f32[4,1,66]{2,1,0:T(1,128)S(1)}, u32[]{:S(2)}, u32[]{:S(2)}) collective-permute-start(f32[4,1,66]{2,1,0:T(1,128)S(1)} %get-tuple-element.377), channel_id=1, source_target_pairs={{0,1},{1,2},{2,3},{3,4},{4,5},{5,6},{6,7},{7,8},{8,9},{9,10},{10,1... | collective-permute-start | bytes 3176 | tf_op jit(solution)/shard_map/while/body/eval_jaxpr/ppermute | solution.py:16
  669.8 6.5 collective-permute-start.1
  678.3 8.5 %collective-permute-start.3 = (f32[4,1,66]{2,1,0:T(1,128)S(1)}, f32[4,1,66]{2,1,0:T(1,128)S(1)}, u32[]{:S(2)}, u32[]{:S(2)}) collective-permute-start(f32[4,1,66]{2,1,0:T(1,128)S(1)} %get-tuple-element.377), channel_id=1, source_target_pairs={{0,1},{1,2},{2,3},{3,4},{4,5},{5,6},{6,7},{7,8},{8,9},{9,10},{10,1... | collective-permute-start | bytes 3176 | tf_op jit(solution)/shard_map/while/body/eval_jaxpr/ppermute | solution.py:16
  689.0 6.5 collective-permute-start.1
  697.5 8.5 %collective-permute-start.3 = (f32[4,1,66]{2,1,0:T(1,128)S(1)}, f32[4,1,66]{2,1,0:T(1,128)S(1)}, u32[]{:S(2)}, u32[]{:S(2)}) collective-permute-start(f32[4,1,66]{2,1,0:T(1,128)S(1)} %get-tuple-element.377), channel_id=1, source_target_pairs={{0,1},{1,2},{2,3},{3,4},{4,5},{5,6},{6,7},{7,8},{8,9},{9,10},{10,1... | collective-permute-start | bytes 3176 | tf_op jit(solution)/shard_map/while/body/eval_jaxpr/ppermute | solution.py:16
  708.2 6.5 collective-permute-start.1
  716.7 8.5 %collective-permute-start.3 = (f32[4,1,66]{2,1,0:T(1,128)S(1)}, f32[4,1,66]{2,1,0:T(1,128)S(1)}, u32[]{:S(2)}, u32[]{:S(2)}) collective-permute-start(f32[4,1,66]{2,1,0:T(1,128)S(1)} %get-tuple-element.377), channel_id=1, source_target_pairs={{0,1},{1,2},{2,3},{3,4},{4,5},{5,6},{6,7},{7,8},{8,9},{9,10},{10,1... | collective-permute-start | bytes 3176 | tf_op jit(solution)/shard_map/while/body/eval_jaxpr/ppermute | solution.py:16
  (33 other events, 667.1 us)
Sparse Core Ops, SparseCore 0:
  364.8 41.5 all-reduce.10
where the time goes:
time: 741 us; the launch traced here: 737 us
  waiting for transfers between devices  284 us (38%)
  starting transfers between devices  214 us (29%)
  other arithmetic  113 us (15%)
  blocking collectives  47.1 us (6%)
  matrix products  38.2 us (5%)
  local copies, waits for them, and re-layouts  22.2 us (3%)
  between operations  15.8 us (2%)
    ppermute x37, waiting for transfers between devices, extended(): lax.ppermute(lax.slice_in_dim(block, block.shape[dim] - width, None, axis...  238 us
    ppermute x37, starting transfers between devices, extended(): lax.ppermute(lax.slice_in_dim(block, block.shape[dim] - width, None, axis...  110 us
    ppermute x37, starting transfers between devices, extended(): lax.ppermute(lax.slice_in_dim(block, 0, width, axis=dim), axis, backward)  104 us
    div x2, other arithmetic, on_device(): iteration_bundle = (xterm + yterm + zterm + equilibrium_emission) / denom  61.9 us
    psum x1, blocking collectives, on_device(): rate_total, cond_total = lax.psum((part_rate, part_cond), 'modes')  47.1 us
    psum x1, waiting for transfers between devices, on_device(): whole_moments = lax.psum(moments, 'modes')  41.6 us
    dot_general x3, matrix products, on_device(): jnp.einsum('fd,fdpxy->pxy', coef, iteration_bundle, precision=highest)  35.5 us
    reduce_sum x1, other arithmetic, on_device(): summed = jnp.sum(iteration_bundle, axis=1)  31.8 us
  transfers between devices with their start and end apart: 75, of which 38 were waited for; matrix products, arithmetic and copies ran while one was open for 1% of the time, Pallas kernels for 0%

commit v1 on v0

--- a/solution.py
+++ b/solution.py
@@ -149,7 +149,7 @@
     ]
     moments = jnp.stack([numer] + fluxes)
     leading_entry_index = lax.axis_index("modes") * tiled_extent
-    whole_moments = lax.psum(moments, "modes")
+    whole_moments = jnp.sum(lax.all_gather(moments, "modes"), axis=0)
     tile_moments = lax.dynamic_slice_in_dim(whole_moments, leading_entry_index, tiled_extent, 3)
     tile_types = lax.dynamic_slice_in_dim(
         node_substance_label, leading_entry_index, tiled_extent, 2

time: 741 us -> 689 us (0.930)
  waiting for transfers between devices: 284 us -> 242 us
  between operations: 15.8 us -> 2.37 us
    psum x1 -> x0, waiting for transfers between devices: 41.6 us -> none  [on_device(): whole_moments = lax.psum(moments, 'modes')]
  transfers between devices with their start and end apart: 75 -> 74, of which waited for: 38 -> 37; matrix products, arithmetic and copies ran while one was open for 1% -> 1% of each run, Pallas kernels for 0% -> 0%
where the time goes in v1:
time: 689 us; the launch traced here: 685 us
  waiting for transfers between devices  242 us (35%)
  starting transfers between devices  212 us (31%)
  other arithmetic  111 us (16%)
  blocking collectives  54.3 us (8%)
  matrix products  38.3 us (6%)
  local copies, waits for them, and re-layouts  21.5 us (3%)
    ppermute x37, waiting for transfers between devices, extended(): lax.ppermute(lax.slice_in_dim(block, block.shape[dim] - width, None, axis...  238 us
    ppermute x37, starting transfers between devices, extended(): lax.ppermute(lax.slice_in_dim(block, block.shape[dim] - width, None, axis...  110 us
    ppermute x37, starting transfers between devices, extended(): lax.ppermute(lax.slice_in_dim(block, 0, width, axis=dim), axis, backward)  102 us
    div x2, other arithmetic, on_device(): iteration_bundle = (xterm + yterm + zterm + equilibrium_emission) / denom  62.3 us
    psum x1, blocking collectives, on_device(): rate_total, cond_total = lax.psum((part_rate, part_cond), 'modes')  47.1 us
    dot_general x3, matrix products, on_device(): jnp.einsum('fd,fdpxy->pxy', coef, iteration_bundle, precision=highest)  35.5 us
    reduce_sum x1, other arithmetic, on_device(): summed = jnp.sum(iteration_bundle, axis=1)  31.8 us
  transfers between devices with their start and end apart: 74, of which 37 were waited for; matrix products, arithmetic and copies ran while one was open for 1% of the time, Pallas kernels for 0%

profile of v1, /device:TPU:22, one launch (start us, length us, event | category | flops | bytes accessed | tf_op | source)
XLA Modules:
  0.0 685.0 jit_solution(4668274299625903013)
XLA Ops:
  9.7 6.8 collective-permute-start.5
  18.3 49.3 %collective-permute-done.4 = f32[10,60,4,1,256]{4,2,3,1,0:T(4,128)S(1)} collective-permute-done((f32[10,60,4,1,256]{4,2,3,1,0:T(4,128)S(1)}, f32[10,60,4,1,256]{4,2,3,1,0:T(4,128)S(1)}, u32[]{:S(2)}, u32[]{:S(2)}) %collective-permute-start.4) | collective-permute-done | bytes 2457632 | tf_op jit(solution)/shard_map/ppermute | solution.py:16
  70.6 6.3 broadcast_in_dim.7
  76.9 31.1 %add_divide_fusion.2 = f32[10,60,4,4,256]{4,2,3,1,0:T(4,128)} fusion(f32[10,60,4,4,256]{4,2,3,1,0:T(4,128)} %broadcast_in_dim.7, f32[10,60,4,1,256]{4,2,3,1,0:T(4,128)} %copy-done.3, f32[10,60,4,1,256]{4,2,3,1,0:T(4,128)S(1)} %collective-permute-done.4, f32[10,4,4,256]{3,1,2,0:T(4,128)S(1)} %copy.13, f32[10,60]{1,0:T(8,128)S(1)} %get-tuple-element.267, ...), kind=kLoop, calls=%fused_computation.49 | loop fusion | flops 39321600 | bytes 24920480 | tf_op jit(solution)/shard_map/div | solution.py:142
  113.2 7.4 %collective-permute-start.7 = (f32[10,60,4,1,256]{4,2,3,1,0:T(4,128)S(1)}, f32[10,60,4,1,256]{4,2,3,1,0:T(4,128)}, u32[]{:S(2)}, u32[]{:S(2)}) collective-permute-start(f32[10,60,4,1,256]{4,2,3,1,0:T(4,128)S(1)} %get-tuple-element.232), channel_id=1, source_target_pairs={{1,0},{2,1},{3,2},{4,3},{5,4},{6,5},{7,6},{8,7},{9,8},{10,9},{11,1... | collective-permute-start | bytes 7372808 | tf_op jit(solution)/shard_map/ppermute | solution.py:19
  120.6 50.6 %collective-permute-done.6 = f32[10,60,4,1,256]{4,2,3,1,0:T(4,128)S(1)} collective-permute-done((f32[10,60,4,1,256]{4,2,3,1,0:T(4,128)S(1)}, f32[10,60,4,1,256]{4,2,3,1,0:T(4,128)S(1)}, u32[]{:S(2)}, u32[]{:S(2)}) %collective-permute-start.6) | collective-permute-done | bytes 2457632 | tf_op jit(solution)/shard_map/ppermute | solution.py:16
  172.4 31.2 %add_divide_fusion.1 = f32[10,60,4,4,256]{4,2,3,1,0:T(4,128)} fusion(f32[10,60,4,4,256]{4,2,3,1,0:T(4,128)} %add_divide_fusion.2, f32[10,60,4,1,256]{4,2,3,1,0:T(4,128)} %collective-permute-done.7, f32[10,60,4,1,256]{4,2,3,1,0:T(4,128)S(1)} %collective-permute-done.6, f32[10,4,4,256]{3,1,2,0:T(4,128)S(1)} %copy.13, f32[10,60]{1,0:T(8,128)S(1)} %get-tuple-element.267, ...), kind=kLoop, calls=%fused_computation.48 | loop fusion | flops 39321600 | bytes 24920480 | tf_op jit(solution)/shard_map/div | solution.py:142
  203.6 5.6 fusion.91
  211.3 7.3 %collective-permute-start.9 = (f32[10,60,4,1,256]{4,2,3,1,0:T(4,128)}, f32[10,60,4,1,256]{4,2,3,1,0:T(4,128)}, u32[]{:S(2)}, u32[]{:S(2)}) collective-permute-start(f32[10,60,4,1,256]{4,2,3,1,0:T(4,128)} %get-tuple-element.230), channel_id=1, source_target_pairs={{1,0},{2,1},{3,2},{4,3},{5,4},{6,5},{7,6},{8,7},{9,8},{10,9},{11,1... | collective-permute-start | bytes 7372808 | tf_op jit(solution)/shard_map/ppermute | solution.py:19
  218.6 47.1 %all-reduce.8 = (f32[3]{0:T(128)S(1)}, f32[3]{0:T(128)S(1)}) all-reduce(f32[3]{0:T(128)S(1)} %get-tuple-element.176, f32[3]{0:T(128)S(1)} %get-tuple-element.175), channel_id=1, replica_groups=mesh['modes'=4,'space'=64] {'modes'}, use_global_device_ids=true, to_apply=%region_4.5 | all-reduce | flops 6 | bytes 48 | tf_op jit(solution)/shard_map/psum | solution.py:107
  270.9 5.1 collective-permute-start.11
  279.4 8.7 %collective-permute-start.13 = (f32[4,1,66]{2,1,0:T(1,128)S(1)}, f32[4,1,66]{2,1,0:T(1,128)S(1)}, u32[]{:S(2)}, u32[]{:S(2)}) collective-permute-start(f32[4,1,66]{2,1,0:T(1,128)S(1)} %get-tuple-element.241), channel_id=1, source_target_pairs={{1,0},{2,1},{3,2},{4,3},{5,4},{6,5},{7,6},{8,7},{9,8},{10,9},{11,1... | collective-permute-start | bytes 3176 | tf_op jit(solution)/shard_map/ppermute | solution.py:19
  290.4 31.8 %fusion.87 = (f32[10,4,4,256]{3,1,2,0:T(4,128)S(1)}, f32[10,60,4,4,256]{4,2,3,1,0:T(4,128)}) fusion(f32[10,4,4,256]{3,1,2,0:T(4,128)S(1)} %copy.13, f32[10,60]{1,0:T(8,128)S(1)} %get-tuple-element.267, f32[10,4,4,256]{3,1,2,0:T(4,128)S(1)} %copy.12, f32[10,60]{1,0:T(8,128)S(1)} %get-tuple-element.269, f32[10,60,4,4,256]{4,2,3,1,0:T(4,128)} %add_divide_fusion.1, ...), kind=kLoop, calls=%fused_computation.194 | loop fusion | flops 41738240 | bytes 25084320 | tf_op jit(solution)/shard_map/reduce_sum | solution.py:143
  322.4 15.9 %fusion.22 = f32[1,4,4,256,1]{3,0,4,2,1:T(1,128)S(1)} fusion(f32[10,60,4,4,256]{4,2,3,1,0:T(4,128)} %get-tuple-element.216, f32[10,60,1,1,1]{1,0,2,3,4:T(8,128)S(1)} %get-tuple-element.256), kind=kOutput, calls=%fused_computation.58 | convolution fusion | flops 29491200 | bytes 9849184 | tf_op jit(solution)/shard_map/fd,fdpxy->pxy/dot_general | solution.py:146
  338.3 9.9 %fusion.20 = f32[1,4,4,256,1]{3,0,4,2,1:T(1,128)S(1)} fusion(f32[10,60,4,4,256]{4,2,3,1,0:T(4,128)S(1)} %copy-done.2, f32[10,60,1,1,1]{1,0,2,3,4:T(8,128)S(1)} %get-tuple-element.273), kind=kOutput, calls=%fused_computation.56 | convolution fusion | flops 29491200 | bytes 9849184 | tf_op jit(solution)/shard_map/fd,fdpxy->pxy/dot_general | solution.py:146
  348.3 9.7 %fusion.18 = f32[1,4,4,256,1]{3,0,4,2,1:T(1,128)S(1)} fusion(f32[10,60,4,4,256]{4,2,3,1,0:T(4,128)S(1)} %copy-done.2, f32[10,60,1,1,1]{1,0,2,3,4:T(8,128)S(1)} %get-tuple-element.270), kind=kOutput, calls=%fused_computation.54 | convolution fusion | flops 29491200 | bytes 9849184 | tf_op jit(solution)/shard_map/fd,fdpxy->pxy/dot_general | solution.py:146
  358.0 7.3 %all-gather = f32[16,4,4,256]{3,2,1,0:T(4,128)S(1)} all-gather(f32[4,4,4,256]{3,2,1,0:T(4,128)S(1)} %pad_maximum_fusion.17), channel_id=2, replica_groups=mesh['modes'=4,'space'=64] {'modes'}, dimensions={0}, use_global_device_ids=true | all-gather | bytes 327680 | tf_op jit(solution)/shard_map/all_gather | solution.py:152
  369.2 312.6 %while.19 = (s32[]{:T(128)}, f32[4,4,64]{2,1,0:T(4,128)S(1)}, f32[4,4,64]{2,1,0:T(4,128)S(1)}, f32[4,4,64]{2,1,0:T(4,128)S(1)}, f32[]{:T(128)}, /*index=5*/f32[4...) while((s32[]{:T(128)}, f32[4,4,64]{2,1,0:T(4,128)S(1)}, ...), condition=%wide.region_9.10_spmd.clone, body=%wide.region_8.9_spmd.clone.sunk | while | flops 68488 | bytes 103667 | solution.py:66
  374.3 4.5 collective-permute-done.1
  378.9 6.0 collective-permute-start.2
  386.9 6.4 collective-permute-done.3
  398.1 4.0 collective-permute-done.1
  408.2 4.4 collective-permute-done.3
  417.3 4.0 collective-permute-done.1
  427.4 4.4 collective-permute-done.3
  436.5 4.0 collective-permute-done.1
  446.6 4.4 collective-permute-done.3
  455.7 4.0 collective-permute-done.1
  465.8 4.4 collective-permute-done.3
  474.9 4.0 collective-permute-done.1
  485.0 4.4 collective-permute-done.3
  494.1 4.0 collective-permute-done.1
  504.2 4.4 collective-permute-done.3
  513.3 4.0 collective-permute-done.1
  523.4 4.4 collective-permute-done.3
  532.5 4.0 collective-permute-done.1
  542.6 4.4 collective-permute-done.3
  551.7 4.0 collective-permute-done.1
  561.8 4.4 collective-permute-done.3
  570.9 4.0 collective-permute-done.1
  581.1 4.4 collective-permute-done.3
  590.2 4.0 collective-permute-done.1
  600.3 4.4 collective-permute-done.3
  609.4 4.0 collective-permute-done.1
  619.5 4.4 collective-permute-done.3
  638.7 4.4 collective-permute-done.3
  657.9 4.4 collective-permute-done.3
  677.1 4.4 collective-permute-done.3
  (256 shorter events, 216.5 us)
Async XLA Ops:
  5.5 62.1 %collective-permute-start.4 = (f32[10,60,4,1,256]{4,2,3,1,0:T(4,128)S(1)}, f32[10,60,4,1,256]{4,2,3,1,0:T(4,128)S(1)}, u32[]{:S(2)}, u32[]{:S(2)}) collective-permute-start(f32[10,60,4,1,256]{4,2,3,1,0:T(4,128)S(1)} %broadcast_in_dim.6), channel_id=1, source_target_pairs={{0,1},{1,2},{2,3},{3,4},{4,5},{5,6},{6,7},{7,8},{8,9},{9,10},{10,1... | collective-permute-start | bytes 7372808 | tf_op jit(solution)/shard_map/ppermute | solution.py:16
  9.7 59.4 %collective-permute-start.5 = (f32[10,60,4,1,256]{4,2,3,1,0:T(4,128)S(1)}, f32[10,60,4,1,256]{4,2,3,1,0:T(4,128)S(1)}, u32[]{:S(2)}, u32[]{:S(2)}) collective-permute-start(f32[10,60,4,1,256]{4,2,3,1,0:T(4,128)S(1)} %broadcast_in_dim.8), channel_id=1, source_target_pairs={{1,0},{2,1},{3,2},{4,3},{5,4},{6,5},{7,6},{8,7},{9,8},{10,9},{11,1... | collective-permute-start | bytes 7372808 | tf_op jit(solution)/shard_map/ppermute | solution.py:19
  111.3 59.9 %collective-permute-start.6 = (f32[10,60,4,1,256]{4,2,3,1,0:T(4,128)S(1)}, f32[10,60,4,1,256]{4,2,3,1,0:T(4,128)S(1)}, u32[]{:S(2)}, u32[]{:S(2)}) collective-permute-start(f32[10,60,4,1,256]{4,2,3,1,0:T(4,128)S(1)} %get-tuple-element.231), channel_id=1, source_target_pairs={{0,1},{1,2},{2,3},{3,4},{4,5},{5,6},{6,7},{7,8},{8,9},{9,10},{10,1... | collective-permute-start | bytes 7372808 | tf_op jit(solution)/shard_map/ppermute | solution.py:16
  113.2 59.1 %collective-permute-start.7 = (f32[10,60,4,1,256]{4,2,3,1,0:T(4,128)S(1)}, f32[10,60,4,1,256]{4,2,3,1,0:T(4,128)}, u32[]{:S(2)}, u32[]{:S(2)}) collective-permute-start(f32[10,60,4,1,256]{4,2,3,1,0:T(4,128)S(1)} %get-tuple-element.232), channel_id=1, source_target_pairs={{1,0},{2,1},{3,2},{4,3},{5,4},{6,5},{7,6},{8,7},{9,8},{10,9},{11,1... | collective-permute-start | bytes 7372808 | tf_op jit(solution)/shard_map/ppermute | solution.py:19
  209.2 81.2 %collective-permute-start.8 = (f32[10,60,4,1,256]{4,2,3,1,0:T(4,128)}, f32[10,60,4,1,256]{4,2,3,1,0:T(4,128)S(1)}, u32[]{:S(2)}, u32[]{:S(2)}) collective-permute-start(f32[10,60,4,1,256]{4,2,3,1,0:T(4,128)} %get-tuple-element.229), channel_id=1, source_target_pairs={{0,1},{1,2},{2,3},{3,4},{4,5},{5,6},{6,7},{7,8},{8,9},{9,10},{10,1... | collective-permute-start | bytes 7372808 | tf_op jit(solution)/shard_map/ppermute | solution.py:16
  211.3 79.1 %collective-permute-start.9 = (f32[10,60,4,1,256]{4,2,3,1,0:T(4,128)}, f32[10,60,4,1,256]{4,2,3,1,0:T(4,128)}, u32[]{:S(2)}, u32[]{:S(2)}) collective-permute-start(f32[10,60,4,1,256]{4,2,3,1,0:T(4,128)} %get-tuple-element.230), channel_id=1, source_target_pairs={{1,0},{2,1},{3,2},{4,3},{5,4},{6,5},{7,6},{8,7},{9,8},{10,9},{11,1... | collective-permute-start | bytes 7372808 | tf_op jit(solution)/shard_map/ppermute | solution.py:19
  269.0 7.1 %collective-permute-start.10 = (f32[4,4,1]{2,1,0:T(4,128)S(1)}, f32[4,4,1]{2,1,0:T(4,128)S(1)}, u32[]{:S(2)}, u32[]{:S(2)}) collective-permute-start(f32[4,4,1]{2,1,0:T(4,128)S(1)} %get-tuple-element.249), channel_id=1, source_target_pairs={{0,64},{64,128},{128,192},{1,65},{65,129},{129,193},{2,66},{66,130... | collective-permute-start | bytes 200 | tf_op jit(solution)/shard_map/ppermute | solution.py:16
  270.9 6.5 collective-permute-start.11
  277.5 12.7 %collective-permute-start.12 = (f32[4,1,66]{2,1,0:T(1,128)S(1)}, f32[4,1,66]{2,1,0:T(1,128)S(1)}, u32[]{:S(2)}, u32[]{:S(2)}) collective-permute-start(f32[4,1,66]{2,1,0:T(1,128)S(1)} %get-tuple-element.242), channel_id=1, source_target_pairs={{0,1},{1,2},{2,3},{3,4},{4,5},{5,6},{6,7},{7,8},{8,9},{9,10},{10,1... | collective-permute-start | bytes 3176 | tf_op jit(solution)/shard_map/ppermute | solution.py:16
  279.4 10.8 %collective-permute-start.13 = (f32[4,1,66]{2,1,0:T(1,128)S(1)}, f32[4,1,66]{2,1,0:T(1,128)S(1)}, u32[]{:S(2)}, u32[]{:S(2)}) collective-permute-start(f32[4,1,66]{2,1,0:T(1,128)S(1)} %get-tuple-element.241), channel_id=1, source_target_pairs={{1,0},{2,1},{3,2},{4,3},{5,4},{6,5},{7,6},{8,7},{9,8},{10,9},{11,1... | collective-permute-start | bytes 3176 | tf_op jit(solution)/shard_map/ppermute | solution.py:19
  372.4 6.5 collective-permute-start.1
  378.9 8.0 %collective-permute-start.2 = (f32[4,1,66]{2,1,0:T(1,128)S(1)}, f32[4,1,66]{2,1,0:T(1,128)S(1)}, u32[]{:S(2)}, u32[]{:S(2)}) collective-permute-start(f32[4,1,66]{2,1,0:T(1,128)S(1)} %get-tuple-element.376), channel_id=1, source_target_pairs={{1,0},{2,1},{3,2},{4,3},{5,4},{6,5},{7,6},{8,7},{9,8},{10,9},{11,1... | collective-permute-start | bytes 3176 | tf_op jit(solution)/shard_map/while/body/eval_jaxpr/ppermute | solution.py:19
  384.9 8.5 %collective-permute-start.3 = (f32[4,1,66]{2,1,0:T(1,128)S(1)}, f32[4,1,66]{2,1,0:T(1,128)S(1)}, u32[]{:S(2)}, u32[]{:S(2)}) collective-permute-start(f32[4,1,66]{2,1,0:T(1,128)S(1)} %get-tuple-element.377), channel_id=1, source_target_pairs={{0,1},{1,2},{2,3},{3,4},{4,5},{5,6},{6,7},{7,8},{8,9},{9,10},{10,1... | collective-permute-start | bytes 3176 | tf_op jit(solution)/shard_map/while/body/eval_jaxpr/ppermute | solution.py:16
  395.6 6.5 collective-permute-start.1
  402.2 6.0 collective-permute-start.2
  404.1 8.5 %collective-permute-start.3 = (f32[4,1,66]{2,1,0:T(1,128)S(1)}, f32[4,1,66]{2,1,0:T(1,128)S(1)}, u32[]{:S(2)}, u32[]{:S(2)}) collective-permute-start(f32[4,1,66]{2,1,0:T(1,128)S(1)} %get-tuple-element.377), channel_id=1, source_target_pairs={{0,1},{1,2},{2,3},{3,4},{4,5},{5,6},{6,7},{7,8},{8,9},{9,10},{10,1... | collective-permute-start | bytes 3176 | tf_op jit(solution)/shard_map/while/body/eval_jaxpr/ppermute | solution.py:16
  414.8 6.5 collective-permute-start.1
  421.4 6.0 collective-permute-start.2
  423.3 8.5 %collective-permute-start.3 = (f32[4,1,66]{2,1,0:T(1,128)S(1)}, f32[4,1,66]{2,1,0:T(1,128)S(1)}, u32[]{:S(2)}, u32[]{:S(2)}) collective-permute-start(f32[4,1,66]{2,1,0:T(1,128)S(1)} %get-tuple-element.377), channel_id=1, source_target_pairs={{0,1},{1,2},{2,3},{3,4},{4,5},{5,6},{6,7},{7,8},{8,9},{9,10},{10,1... | collective-permute-start | bytes 3176 | tf_op jit(solution)/shard_map/while/body/eval_jaxpr/ppermute | solution.py:16
  434.1 6.5 collective-permute-start.1
  442.5 8.5 %collective-permute-start.3 = (f32[4,1,66]{2,1,0:T(1,128)S(1)}, f32[4,1,66]{2,1,0:T(1,128)S(1)}, u32[]{:S(2)}, u32[]{:S(2)}) collective-permute-start(f32[4,1,66]{2,1,0:T(1,128)S(1)} %get-tuple-element.377), channel_id=1, source_target_pairs={{0,1},{1,2},{2,3},{3,4},{4,5},{5,6},{6,7},{7,8},{8,9},{9,10},{10,1... | collective-permute-start | bytes 3176 | tf_op jit(solution)/shard_map/while/body/eval_jaxpr/ppermute | solution.py:16
  453.3 6.5 collective-permute-start.1
  459.8 6.0 collective-permute-start.2
  461.8 8.5 %collective-permute-start.3 = (f32[4,1,66]{2,1,0:T(1,128)S(1)}, f32[4,1,66]{2,1,0:T(1,128)S(1)}, u32[]{:S(2)}, u32[]{:S(2)}) collective-permute-start(f32[4,1,66]{2,1,0:T(1,128)S(1)} %get-tuple-element.377), channel_id=1, source_target_pairs={{0,1},{1,2},{2,3},{3,4},{4,5},{5,6},{6,7},{7,8},{8,9},{9,10},{10,1... | collective-permute-start | bytes 3176 | tf_op jit(solution)/shard_map/while/body/eval_jaxpr/ppermute | solution.py:16
  472.5 6.5 collective-permute-start.1
  479.0 6.0 collective-permute-start.2
  481.0 8.5 %collective-permute-start.3 = (f32[4,1,66]{2,1,0:T(1,128)S(1)}, f32[4,1,66]{2,1,0:T(1,128)S(1)}, u32[]{:S(2)}, u32[]{:S(2)}) collective-permute-start(f32[4,1,66]{2,1,0:T(1,128)S(1)} %get-tuple-element.377), channel_id=1, source_target_pairs={{0,1},{1,2},{2,3},{3,4},{4,5},{5,6},{6,7},{7,8},{8,9},{9,10},{10,1... | collective-permute-start | bytes 3176 | tf_op jit(solution)/shard_map/while/body/eval_jaxpr/ppermute | solution.py:16
  491.7 6.5 collective-permute-start.1
  500.2 8.5 %collective-permute-start.3 = (f32[4,1,66]{2,1,0:T(1,128)S(1)}, f32[4,1,66]{2,1,0:T(1,128)S(1)}, u32[]{:S(2)}, u32[]{:S(2)}) collective-permute-start(f32[4,1,66]{2,1,0:T(1,128)S(1)} %get-tuple-element.377), channel_id=1, source_target_pairs={{0,1},{1,2},{2,3},{3,4},{4,5},{5,6},{6,7},{7,8},{8,9},{9,10},{10,1... | collective-permute-start | bytes 3176 | tf_op jit(solution)/shard_map/while/body/eval_jaxpr/ppermute | solution.py:16
  510.9 6.5 collective-permute-start.1
  517.5 6.0 collective-permute-start.2
  519.4 8.5 %collective-permute-start.3 = (f32[4,1,66]{2,1,0:T(1,128)S(1)}, f32[4,1,66]{2,1,0:T(1,128)S(1)}, u32[]{:S(2)}, u32[]{:S(2)}) collective-permute-start(f32[4,1,66]{2,1,0:T(1,128)S(1)} %get-tuple-element.377), channel_id=1, source_target_pairs={{0,1},{1,2},{2,3},{3,4},{4,5},{5,6},{6,7},{7,8},{8,9},{9,10},{10,1... | collective-permute-start | bytes 3176 | tf_op jit(solution)/shard_map/while/body/eval_jaxpr/ppermute | solution.py:16
  530.1 6.5 collective-permute-start.1
  538.6 8.5 %collective-permute-start.3 = (f32[4,1,66]{2,1,0:T(1,128)S(1)}, f32[4,1,66]{2,1,0:T(1,128)S(1)}, u32[]{:S(2)}, u32[]{:S(2)}) collective-permute-start(f32[4,1,66]{2,1,0:T(1,128)S(1)} %get-tuple-element.377), channel_id=1, source_target_pairs={{0,1},{1,2},{2,3},{3,4},{4,5},{5,6},{6,7},{7,8},{8,9},{9,10},{10,1... | collective-permute-start | bytes 3176 | tf_op jit(solution)/shard_map/while/body/eval_jaxpr/ppermute | solution.py:16
  549.3 6.5 collective-permute-start.1
  557.8 8.5 %collective-permute-start.3 = (f32[4,1,66]{2,1,0:T(1,128)S(1)}, f32[4,1,66]{2,1,0:T(1,128)S(1)}, u32[]{:S(2)}, u32[]{:S(2)}) collective-permute-start(f32[4,1,66]{2,1,0:T(1,128)S(1)} %get-tuple-element.377), channel_id=1, source_target_pairs={{0,1},{1,2},{2,3},{3,4},{4,5},{5,6},{6,7},{7,8},{8,9},{9,10},{10,1... | collective-permute-start | bytes 3176 | tf_op jit(solution)/shard_map/while/body/eval_jaxpr/ppermute | solution.py:16
  568.5 6.5 collective-permute-start.1
  577.0 8.5 %collective-permute-start.3 = (f32[4,1,66]{2,1,0:T(1,128)S(1)}, f32[4,1,66]{2,1,0:T(1,128)S(1)}, u32[]{:S(2)}, u32[]{:S(2)}) collective-permute-start(f32[4,1,66]{2,1,0:T(1,128)S(1)} %get-tuple-element.377), channel_id=1, source_target_pairs={{0,1},{1,2},{2,3},{3,4},{4,5},{5,6},{6,7},{7,8},{8,9},{9,10},{10,1... | collective-permute-start | bytes 3176 | tf_op jit(solution)/shard_map/while/body/eval_jaxpr/ppermute | solution.py:16
  587.7 6.5 collective-permute-start.1
  596.2 8.5 %collective-permute-start.3 = (f32[4,1,66]{2,1,0:T(1,128)S(1)}, f32[4,1,66]{2,1,0:T(1,128)S(1)}, u32[]{:S(2)}, u32[]{:S(2)}) collective-permute-start(f32[4,1,66]{2,1,0:T(1,128)S(1)} %get-tuple-element.377), channel_id=1, source_target_pairs={{0,1},{1,2},{2,3},{3,4},{4,5},{5,6},{6,7},{7,8},{8,9},{9,10},{10,1... | collective-permute-start | bytes 3176 | tf_op jit(solution)/shard_map/while/body/eval_jaxpr/ppermute | solution.py:16
  606.9 6.5 collective-permute-start.1
  615.4 8.5 %collective-permute-start.3 = (f32[4,1,66]{2,1,0:T(1,128)S(1)}, f32[4,1,66]{2,1,0:T(1,128)S(1)}, u32[]{:S(2)}, u32[]{:S(2)}) collective-permute-start(f32[4,1,66]{2,1,0:T(1,128)S(1)} %get-tuple-element.377), channel_id=1, source_target_pairs={{0,1},{1,2},{2,3},{3,4},{4,5},{5,6},{6,7},{7,8},{8,9},{9,10},{10,1... | collective-permute-start | bytes 3176 | tf_op jit(solution)/shard_map/while/body/eval_jaxpr/ppermute | solution.py:16
  626.2 6.5 collective-permute-start.1
  634.6 8.5 %collective-permute-start.3 = (f32[4,1,66]{2,1,0:T(1,128)S(1)}, f32[4,1,66]{2,1,0:T(1,128)S(1)}, u32[]{:S(2)}, u32[]{:S(2)}) collective-permute-start(f32[4,1,66]{2,1,0:T(1,128)S(1)} %get-tuple-element.377), channel_id=1, source_target_pairs={{0,1},{1,2},{2,3},{3,4},{4,5},{5,6},{6,7},{7,8},{8,9},{9,10},{10,1... | collective-permute-start | bytes 3176 | tf_op jit(solution)/shard_map/while/body/eval_jaxpr/ppermute | solution.py:16
  645.4 6.5 collective-permute-start.1
  653.9 8.5 %collective-permute-start.3 = (f32[4,1,66]{2,1,0:T(1,128)S(1)}, f32[4,1,66]{2,1,0:T(1,128)S(1)}, u32[]{:S(2)}, u32[]{:S(2)}) collective-permute-start(f32[4,1,66]{2,1,0:T(1,128)S(1)} %get-tuple-element.377), channel_id=1, source_target_pairs={{0,1},{1,2},{2,3},{3,4},{4,5},{5,6},{6,7},{7,8},{8,9},{9,10},{10,1... | collective-permute-start | bytes 3176 | tf_op jit(solution)/shard_map/while/body/eval_jaxpr/ppermute | solution.py:16
  664.6 6.5 collective-permute-start.1
  673.1 8.5 %collective-permute-start.3 = (f32[4,1,66]{2,1,0:T(1,128)S(1)}, f32[4,1,66]{2,1,0:T(1,128)S(1)}, u32[]{:S(2)}, u32[]{:S(2)}) collective-permute-start(f32[4,1,66]{2,1,0:T(1,128)S(1)} %get-tuple-element.377), channel_id=1, source_target_pairs={{0,1},{1,2},{2,3},{3,4},{4,5},{5,6},{6,7},{7,8},{8,9},{9,10},{10,1... | collective-permute-start | bytes 3176 | tf_op jit(solution)/shard_map/while/body/eval_jaxpr/ppermute | solution.py:16
  (32 other events, 586.0 us)
